TPU v7x, 256 devices: a whole 4x4x8 slice. The times are simulated.
256 devices in a mesh: ctx: 64 (over z, y, x_lo), tp: 4 (over x_hi, core).
Axes of the slice: x: 4 (x_hi: 2, x_lo: 2; x = x_hi * 2 + x_lo), y: 4, z: 8, core: 2. Of those that a mesh axis runs over, the one named last changes fastest.
Arguments:
- key_act: bfloat16 [16384, 2048], P('ctx', 'tp'), may hold values from -6 to 6
- value_act: bfloat16 [16384, 2048], P('ctx', 'tp'), may hold values from -6 to 6
- query_act: bfloat16 [16384, 2048], P('ctx', 'tp'), may hold values from -6 to 6
- grad_out: bfloat16 [16384, 2048], P('ctx', 'tp'), may hold values from -6 to 6
- long_filter: bfloat16 [16384, 2048], P('ctx', 'tp'), may hold values from -6 to 6
- w_key: bfloat16 [2048, 2048], P(None, 'tp'), may hold values from -0.125 to 0.125
- w_query: bfloat16 [2048, 2048], P(None, 'tp'), may hold values from -0.125 to 0.125
- w_value: bfloat16 [2048, 2048], P(None, 'tp'), may hold values from -0.125 to 0.125
Outputs:
- grad_input: bfloat16 [16384, 2048], P('ctx', 'tp')
- grad_filter: bfloat16 [16384, 2048], P('ctx', 'tp')
All inputs are finite; a program needn't handle non-finite values.
Results may differ from a plain program's by a relative error of at most 0.025.
Values may be sent and summed in bfloat16 or wider, within the bound.
A program may use at most 128 MiB of HBM per device.

v0:
```python
import functools
import math

import jax
import jax.numpy as jnp
import numpy as np
from jax import lax
from jax.experimental import pallas as pl
from jax.experimental.pallas import tpu as pltpu
from jax.sharding import PartitionSpec as P

f32 = jnp.float32
bf16 = jnp.bfloat16
BLOCKS = 64
CH = 8
LEN = 256
ROWS = BLOCKS * CH
WIDTH = 512
D_OUT = 2048
HALF = 256


def tables():
    total = BLOCKS * LEN
    k = np.arange(BLOCKS)
    b = np.arange(LEN)
    first = np.exp(-2j * np.pi * np.outer(k + 0.25, k) / BLOCKS)
    twist = np.exp(-2j * np.pi * np.outer(k + 0.25, b) / total)
    second = np.exp(-2j * np.pi * np.outer(b, b) / LEN)
    eye = np.eye(CH)
    fwd1 = np.kron(np.concatenate([first.real, first.imag]), eye)
    scale = 1.0 / (total * math.sqrt(total))
    inv1 = np.kron(np.concatenate([first.real.T, first.imag.T], 1), eye) * scale
    fwd2 = np.block([[second.real, second.imag], [-second.imag, second.real]])
    inv2 = np.block([[second.real, -second.imag], [second.imag, second.real]])
    cast = lambda a, t: jnp.asarray(np.asarray(a, np.float32)).astype(t)
    rep = lambda a: np.repeat(a, CH, 0)
    return (
        cast(fwd1, bf16),
        cast(fwd2, bf16),
        cast(inv2, bf16),
        cast(inv1, bf16),
        cast(rep(twist.real), f32),
        cast(rep(twist.imag), f32),
        cast(np.eye(HALF), bf16),
    )


def dot(a, b):
    return jnp.dot(a, b, preferred_element_type=f32)


def dot_nt(a, b):
    return lax.dot_general(a, b, (((1,), (1,)), ((), ())), preferred_element_type=f32)


def partner(me, i):
    z, y, x = me // 8, (me // 2) % 4, me % 2
    dz, r = i % 8, i // 8
    return ((z + dz) % 8) * 8 + ((y + r // 2) % 4) * 2 + (x + r % 2) % 2


def kernel(
    key_h, val_h, qry_h, gout_h, filt_h, wk_h, wq_h, wv_h,
    fwd1_h, fwd2_h, inv2_h, inv1_h, twr_h, twi_h, eye_h,
    gin_ref, gfil_ref,
    key, val, qry, gout, filt, wk, wq, wv,
    fwd1, fwd2, inv2, inv1, twr, twi, eye,
    key_t, val_t, gout_t,
    send, recv, xbuf, spec, ubuf, gbuf, acc,
    sib_out, sib_in, far_out, far_in, fin,
    in_sem, send_sem, recv_sem, rs_send, rs_recv,
):
    me = lax.axis_index("ctx")
    tp = lax.axis_index("tp")
    core = tp % 2
    sib = tp + 1 - 2 * core
    far = (tp + 2) % 4
    diag = 3 - tp

    pairs = [
        (filt_h, filt), (eye_h, eye), (qry_h, qry), (gout_h, gout), (key_h, key), (val_h, val),
        (fwd1_h, fwd1), (twr_h, twr), (twi_h, twi), (fwd2_h, fwd2), (inv2_h, inv2), (inv1_h, inv1),
        (wk_h, wk), (wv_h, wv), (wq_h, wq),
    ]
    loads = [pltpu.make_async_copy(s, d, in_sem.at[n]) for n, (s, d) in enumerate(pairs)]
    for load in loads:
        load.start()

    barrier = pltpu.get_barrier_semaphore()
    for t in (sib, far):
        pl.semaphore_signal(barrier, inc=1, device_id={"tp": t})

    @pl.loop(1, BLOCKS)
    def _(i):
        pl.semaphore_signal(barrier, inc=1, device_id={"ctx": partner(me, i)})

    def flip(src, h):
        return dot_nt(eye[...], src[:, pl.ds(h * HALF, HALF)])

    def post(n):
        pltpu.make_async_copy(send.at[n, me], recv.at[n, me], recv_sem.at[n]).start()

        @pl.loop(1, BLOCKS)
        def _(i):
            d = partner(me, i)
            pltpu.make_async_remote_copy(
                send.at[n, d], recv.at[n, me], send_sem.at[n], recv_sem.at[n],
                device_id={"ctx": d},
            ).start()

    def arrived(n):
        pltpu.make_async_copy(recv.at[n], recv.at[n], recv_sem.at[n]).wait()

    def put_send(n, h, values):
        send[n, pl.ds(h * 32, 32)] = values.reshape(32, CH, LEN).astype(bf16)

    def get_recv(n):
        return recv[n].astype(f32).reshape(ROWS, LEN)

    loads[0].wait()
    loads[1].wait()
    for h in range(2):
        put_send(0, h, flip(filt, h))
    pl.semaphore_wait(barrier, BLOCKS + 1)
    post(0)

    loads[2].wait()
    loads[3].wait()
    for h in range(2):
        rows = pl.ds(h * HALF, HALF)
        g = flip(gout, h)
        gout_t[rows, :] = g.astype(bf16)
        put_send(1, h, flip(qry, h) * g)
    post(1)

    loads[4].wait()
    loads[5].wait()
    for h in range(2):
        rows = pl.ds(h * HALF, HALF)
        a = flip(key, h)
        b = flip(val, h)
        key_t[rows, :] = a.astype(bf16)
        val_t[rows, :] = b.astype(bf16)
        put_send(2, h, a * b)
    post(2)

    def forward(n):
        xbuf[...] = get_recv(n).astype(bf16)

        @pl.loop(0, 2)
        def _(i):
            m = pl.multiple_of(i * HALF, HALF)
            rows = pl.ds(m, HALF)
            yr = dot(fwd1[rows, :], xbuf[...])
            yi = dot(fwd1[pl.ds(m + ROWS, HALF), :], xbuf[...])
            c, s = twr[rows, :], twi[rows, :]
            t = jnp.concatenate([yr * c - yi * s, yr * s + yi * c], axis=1).astype(bf16)
            spec[n, rows, :] = dot(t, fwd2[...])

    def inverse(na, nb, conj, out):
        @pl.loop(0, 2)
        def _(i):
            m = pl.multiple_of(i * HALF, HALF)
            rows = pl.ds(m, HALF)
            ar, ai = spec[na, rows, :LEN], spec[na, rows, LEN:]
            br, bi = spec[nb, rows, :LEN], spec[nb, rows, LEN:]
            if conj:
                yr, yi = ar * br + ai * bi, ai * br - ar * bi
            else:
                yr, yi = ar * br - ai * bi, ar * bi + ai * br
            t = dot(jnp.concatenate([yr, yi], axis=1).astype(bf16), inv2[...])
            tr, ti = t[:, :LEN], t[:, LEN:]
            c, s = twr[rows, :], twi[rows, :]
            ubuf[rows, :] = (tr * c + ti * s).astype(bf16)
            ubuf[pl.ds(m + ROWS, HALF), :] = (ti * c - tr * s).astype(bf16)

        @pl.loop(0, 2)
        def _(i):
            m = pl.multiple_of(i * HALF, HALF)
            y = dot(inv1[pl.ds(m, HALF), :], ubuf[...])
            send[out, pl.ds(i * 32, 32)] = y.reshape(32, CH, LEN).astype(bf16)

    for load in loads[6:12]:
        load.wait()
    arrived(0)
    forward(0)
    arrived(1)
    forward(1)
    inverse(1, 0, True, 3)
    post(3)
    arrived(2)
    forward(2)
    inverse(2, 0, False, 4)
    post(4)
    inverse(1, 2, True, 5)
    post(5)

    for load in loads[12:]:
        load.wait()
    arrived(3)
    back = get_recv(3)
    gbuf[0] = (back * val_t[...].astype(f32)).astype(bf16)
    gbuf[1] = (back * key_t[...].astype(f32)).astype(bf16)

    @pl.loop(0, D_OUT // HALF)
    def _(i):
        rows = pl.ds(pl.multiple_of(i * HALF, HALF), HALF)
        acc[rows, :] = dot(wk[rows, :], gbuf[0]) + dot(wv[rows, :], gbuf[1])

    arrived(4)
    gbuf[2] = (get_recv(4) * gout_t[...].astype(f32)).astype(bf16)

    def term(t):
        rows = pl.ds(pl.multiple_of(t * WIDTH, WIDTH), WIDTH)
        return acc[rows, :] + dot(wq[rows, :], gbuf[2])

    def to_sib(n):
        return pltpu.make_async_remote_copy(
            sib_out.at[n], sib_in.at[n], rs_send.at[n], rs_recv.at[n], device_id={"tp": sib}
        )

    to_far = pltpu.make_async_remote_copy(
        far_out, far_in, rs_send.at[2], rs_recv.at[2], device_id={"tp": far}
    )
    sib_out[0] = term(diag).astype(bf16)
    to_sib(0).start()
    mine = term(far)
    to_sib(0).wait_recv()
    far_out[...] = (mine + sib_in[0].astype(f32)).astype(bf16)
    to_far.start()
    sib_out[1] = term(sib).astype(bf16)
    to_sib(1).start()
    own = term(tp)
    to_sib(1).wait_recv()
    acc[pl.ds(0, WIDTH), :] = own + sib_in[1].astype(f32)

    arrived(5)
    gfil_ref[...] = dot_nt(eye[...], get_recv(5).astype(bf16)).astype(bf16)
    to_far.wait_recv()
    fin[...] = (acc[pl.ds(0, WIDTH), :] + far_in[...].astype(f32)).astype(bf16)
    gin_ref[...] = dot_nt(eye[...], fin[...]).astype(bf16)

    for n in range(6):
        some = send.at[n, pl.ds(0, BLOCKS - 1)]
        pltpu.make_async_copy(some, some, send_sem.at[n]).wait()
    to_sib(0).wait_send()
    to_sib(1).wait_send()
    to_far.wait_send()


def per_device(key_act, value_act, query_act, grad_out, long_filter, w_key, w_query, w_value):
    consts = tables()
    act = lambda: pltpu.VMEM((LEN, WIDTH), bf16)
    weight = lambda: pltpu.VMEM((D_OUT, WIDTH), bf16)
    turned = lambda: pltpu.VMEM((WIDTH, LEN), bf16)
    dma = pltpu.SemaphoreType.DMA
    return pl.pallas_call(
        kernel,
        out_shape=(jax.ShapeDtypeStruct((LEN, WIDTH), bf16),) * 2,
        in_specs=[pl.BlockSpec(memory_space=pl.ANY)] * 15,
        out_specs=[pl.BlockSpec(memory_space=pltpu.VMEM)] * 2,
        scratch_shapes=[act()] * 5
        + [weight()] * 3
        + [pltpu.VMEM(c.shape, c.dtype) for c in consts]
        + [turned()] * 3
        + [
            pltpu.VMEM((6, BLOCKS, CH, LEN), bf16),
            pltpu.VMEM((6, BLOCKS, CH, LEN), bf16),
            pltpu.VMEM((ROWS, LEN), bf16),
            pltpu.VMEM((3, ROWS, 2 * LEN), f32),
            pltpu.VMEM((2 * ROWS, LEN), bf16),
            pltpu.VMEM((3, WIDTH, LEN), bf16),
            pltpu.VMEM((D_OUT, LEN), f32),
            pltpu.VMEM((2, WIDTH, LEN), bf16),
            pltpu.VMEM((2, WIDTH, LEN), bf16),
            turned(),
            turned(),
            turned(),
            dma((15,)),
            dma((6,)),
            dma((6,)),
            dma((3,)),
            dma((3,)),
        ],
        compiler_params=pltpu.CompilerParams(
            collective_id=1, has_side_effects=True, vmem_limit_bytes=56 * 2**20
        ),
    )(key_act, value_act, query_act, grad_out, long_filter, w_key, w_query, w_value, *consts)


def solution(mesh):
    placed = (P("ctx", "tp"),) * 5 + (P(None, "tp"),) * 3
    return jax.shard_map(
        per_device,
        mesh=mesh,
        in_specs=placed,
        out_specs=(P("ctx", "tp"), P("ctx", "tp")),
        check_vma=False,
    )
```

profile of v0, /device:TPU:1, one launch (start us, length us, event | category | flops | bytes accessed | tf_op | source)
XLA Modules:
  0.0 64.9 jit_solution(2503297654991731983)
XLA Ops:
  0.6 60.9 %shard_map.158 = (bf16[256,512]{1,0:T(8,128)(2,1)}, bf16[256,512]{1,0:T(8,128)(2,1)}) custom-call(bf16[256,512]{1,0:T(8,128)(2,1)} %key_h.1, bf16[256,512]{1,0:T(8,128)(2,1)} %val_h.1, bf16[256,512]{1,0:T(8,128)(2,1)} %qry_h.1, bf16[256,512]{1,0:T(8,128)(2,1)} %gout_h.1, bf16[256,512]{1,0:T(8,128)(2,1)} %filt_h.1, bf16[2048,512]{1,0:T(8,128)(2,1)} %wk_h.1, ...), custom_call_target="tpu_custom_call" | custom-call | tf_op jit(solution)/shard_map/pallas_call | solution.py:258
  61.5 1.7 %copy.19 = bf16[256,512]{1,0:T(8,128)(2,1)} copy(bf16[256,512]{1,0:T(8,128)(2,1)} %get-tuple-element.4) | data formatting | bytes 524288
  63.2 1.7 %copy.20 = bf16[256,512]{1,0:T(8,128)(2,1)} copy(bf16[256,512]{1,0:T(8,128)(2,1)} %get-tuple-element.5) | data formatting | bytes 524288
where the time goes:
time: 65 us; the launch traced here: 64.9 us
  Pallas kernels  60.9 us (94%)
  local copies, waits for them, and re-layouts  3.34 us (5%)
    pallas_call x1, Pallas kernels, per_device(): pl.pallas_call(kernel, out_shape=(jax.ShapeDtypeStruct((LEN, WIDTH), bf16...  60.9 us
    unnamed x2, local copies, waits for them, and re-layouts  3.34 us

commit v1 on v0

--- a/solution.py
+++ b/solution.py
@@ -56,8 +56,11 @@
 
 def partner(me, i):
     z, y, x = me // 8, (me // 2) % 4, me % 2
-    dz, r = i % 8, i // 8
-    return ((z + dz) % 8) * 8 + ((y + r // 2) % 4) * 2 + (x + r % 2) % 2
+    m, r = i % 8, i // 8
+    n = r // 2
+    dz = 4 + ((m + 1) // 2) * (1 - 2 * (m % 2))
+    dy = 2 + ((n + 1) // 2) * (1 - 2 * (n % 2))
+    return ((z + dz) % 8) * 8 + ((y + dy) % 4) * 2 + (x + 1 - r % 2) % 2
 
 
 def kernel(
@@ -68,7 +71,7 @@
     fwd1, fwd2, inv2, inv1, twr, twi, eye,
     key_t, val_t, gout_t,
     send, recv, xbuf, spec, ubuf, gbuf, acc,
-    sib_out, sib_in, far_out, far_in, fin,
+    sib_out, sib_in, far_out, far_in,
     in_sem, send_sem, recv_sem, rs_send, rs_recv,
 ):
     me = lax.axis_index("ctx")
@@ -91,7 +94,7 @@
     for t in (sib, far):
         pl.semaphore_signal(barrier, inc=1, device_id={"tp": t})
 
-    @pl.loop(1, BLOCKS)
+    @pl.loop(0, BLOCKS - 1)
     def _(i):
         pl.semaphore_signal(barrier, inc=1, device_id={"ctx": partner(me, i)})
 
@@ -101,7 +104,7 @@
     def post(n):
         pltpu.make_async_copy(send.at[n, me], recv.at[n, me], recv_sem.at[n]).start()
 
-        @pl.loop(1, BLOCKS)
+        @pl.loop(0, BLOCKS - 1)
         def _(i):
             d = partner(me, i)
             pltpu.make_async_remote_copy(
@@ -208,45 +211,63 @@
         rows = pl.ds(pl.multiple_of(i * HALF, HALF), HALF)
         acc[rows, :] = dot(wk[rows, :], gbuf[0]) + dot(wv[rows, :], gbuf[1])
 
+    def to_sib(n, h):
+        return pltpu.make_async_remote_copy(
+            sib_out.at[n, h], sib_in.at[n, h], rs_send.at[n, h], rs_recv.at[n, h],
+            device_id={"tp": sib},
+        )
+
+    def to_far(h):
+        return pltpu.make_async_remote_copy(
+            far_out.at[h], far_in.at[h], rs_send.at[2, h], rs_recv.at[2, h], device_id={"tp": far}
+        )
+
+    def rows_of(t, h):
+        return pl.ds(pl.multiple_of(t * WIDTH + h * HALF, HALF), HALF)
+
+    def term(t, h):
+        rows = rows_of(t, h)
+        return acc[rows, :] + dot(wq[rows, :], gbuf[2])
+
     arrived(4)
     gbuf[2] = (get_recv(4) * gout_t[...].astype(f32)).astype(bf16)
-
-    def term(t):
-        rows = pl.ds(pl.multiple_of(t * WIDTH, WIDTH), WIDTH)
-        return acc[rows, :] + dot(wq[rows, :], gbuf[2])
-
-    def to_sib(n):
-        return pltpu.make_async_remote_copy(
-            sib_out.at[n], sib_in.at[n], rs_send.at[n], rs_recv.at[n], device_id={"tp": sib}
-        )
-
-    to_far = pltpu.make_async_remote_copy(
-        far_out, far_in, rs_send.at[2], rs_recv.at[2], device_id={"tp": far}
-    )
-    sib_out[0] = term(diag).astype(bf16)
-    to_sib(0).start()
-    mine = term(far)
-    to_sib(0).wait_recv()
-    far_out[...] = (mine + sib_in[0].astype(f32)).astype(bf16)
-    to_far.start()
-    sib_out[1] = term(sib).astype(bf16)
-    to_sib(1).start()
-    own = term(tp)
-    to_sib(1).wait_recv()
-    acc[pl.ds(0, WIDTH), :] = own + sib_in[1].astype(f32)
-
+    for h in range(2):
+        sib_out[0, h] = term(diag, h).astype(bf16)
+        to_sib(0, h).start()
+    for h in range(2):
+        mine = term(far, h)
+        to_sib(0, h).wait_recv()
+        far_out[h] = (mine + sib_in[0, h].astype(f32)).astype(bf16)
+        to_far(h).start()
+    for h in range(2):
+        sib_out[1, h] = term(sib, h).astype(bf16)
+        to_sib(1, h).start()
+    for h in range(2):
+        acc[rows_of(tp, h), :] = term(tp, h)
+    for h in range(2):
+        to_sib(1, h).wait_recv()
+        acc[rows_of(tp, h), :] += sib_in[1, h].astype(f32)
     arrived(5)
-    gfil_ref[...] = dot_nt(eye[...], get_recv(5).astype(bf16)).astype(bf16)
-    to_far.wait_recv()
-    fin[...] = (acc[pl.ds(0, WIDTH), :] + far_in[...].astype(f32)).astype(bf16)
-    gin_ref[...] = dot_nt(eye[...], fin[...]).astype(bf16)
+    gfil_ref[...] = get_recv(5).astype(bf16)
+    for h in range(2):
+        to_far(h).wait_recv()
+        gin_ref[pl.ds(h * HALF, HALF), :] = (acc[rows_of(tp, h), :] + far_in[h].astype(f32)).astype(bf16)
 
     for n in range(6):
         some = send.at[n, pl.ds(0, BLOCKS - 1)]
         pltpu.make_async_copy(some, some, send_sem.at[n]).wait()
-    to_sib(0).wait_send()
-    to_sib(1).wait_send()
-    to_far.wait_send()
+    for h in range(2):
+        to_sib(0, h).wait_send()
+        to_sib(1, h).wait_send()
+        to_far(h).wait_send()
+
+
+def turn(gin_t, gfil_t, gin_ref, gfil_ref):
+    row = lax.broadcasted_iota(jnp.int32, (LEN, LEN), 0)
+    col = lax.broadcasted_iota(jnp.int32, (LEN, LEN), 1)
+    eye = jnp.where(row == col, 1.0, 0.0).astype(bf16)
+    gin_ref[...] = dot_nt(eye, gin_t[...]).astype(bf16)
+    gfil_ref[...] = dot_nt(eye, gfil_t[...]).astype(bf16)
 
 
 def per_device(key_act, value_act, query_act, grad_out, long_filter, w_key, w_query, w_value):
@@ -255,9 +276,9 @@
     weight = lambda: pltpu.VMEM((D_OUT, WIDTH), bf16)
     turned = lambda: pltpu.VMEM((WIDTH, LEN), bf16)
     dma = pltpu.SemaphoreType.DMA
-    return pl.pallas_call(
+    gin_t, gfil_t = pl.pallas_call(
         kernel,
-        out_shape=(jax.ShapeDtypeStruct((LEN, WIDTH), bf16),) * 2,
+        out_shape=(jax.ShapeDtypeStruct((WIDTH, LEN), bf16),) * 2,
         in_specs=[pl.BlockSpec(memory_space=pl.ANY)] * 15,
         out_specs=[pl.BlockSpec(memory_space=pltpu.VMEM)] * 2,
         scratch_shapes=[act()] * 5
@@ -272,21 +293,26 @@
             pltpu.VMEM((2 * ROWS, LEN), bf16),
             pltpu.VMEM((3, WIDTH, LEN), bf16),
             pltpu.VMEM((D_OUT, LEN), f32),
-            pltpu.VMEM((2, WIDTH, LEN), bf16),
-            pltpu.VMEM((2, WIDTH, LEN), bf16),
-            turned(),
-            turned(),
-            turned(),
+            pltpu.VMEM((2, 2, HALF, LEN), bf16),
+            pltpu.VMEM((2, 2, HALF, LEN), bf16),
+            pltpu.VMEM((2, HALF, LEN), bf16),
+            pltpu.VMEM((2, HALF, LEN), bf16),
             dma((15,)),
             dma((6,)),
             dma((6,)),
-            dma((3,)),
-            dma((3,)),
+            dma((3, 2)),
+            dma((3, 2)),
         ],
         compiler_params=pltpu.CompilerParams(
             collective_id=1, has_side_effects=True, vmem_limit_bytes=56 * 2**20
         ),
     )(key_act, value_act, query_act, grad_out, long_filter, w_key, w_query, w_value, *consts)
+    return pl.pallas_call(
+        turn,
+        out_shape=(jax.ShapeDtypeStruct((LEN, WIDTH), bf16),) * 2,
+        in_specs=[pl.BlockSpec(memory_space=pltpu.VMEM)] * 2,
+        out_specs=[pl.BlockSpec(memory_space=pltpu.VMEM)] * 2,
+    )(gin_t, gfil_t)
 
 
 def solution(mesh):

time: 65 us -> 59.7 us (0.918)
  local copies, waits for them, and re-layouts: 3.34 us -> 0 us
  Pallas kernels: 60.9 us -> 59 us
    unnamed x2 -> x0, local copies, waits for them, and re-layouts: 3.34 us -> none
    pallas_call x1 -> x2, Pallas kernels: 60.9 us -> 59 us  [the longest x1 56.9 us: per_device(): pl.pallas_call(kernel, out_shape=(jax.ShapeDtypeStruct((WIDTH, LEN), bf16...]
where the time goes in v1:
time: 59.7 us; the launch traced here: 59.6 us
  Pallas kernels  59 us (99%)
  between operations  0.64 us (1%)
    pallas_call x1, Pallas kernels, per_device(): pl.pallas_call(kernel, out_shape=(jax.ShapeDtypeStruct((WIDTH, LEN), bf16...  56.9 us
    pallas_call x1, Pallas kernels, per_device(): pl.pallas_call(turn, out_shape=(jax.ShapeDtypeStruct((LEN, WIDTH), bf16),...  2.08 us

profile of v1, /device:TPU:1, one launch (start us, length us, event | category | flops | bytes accessed | tf_op | source)
XLA Modules:
  0.0 59.6 jit_solution(8128983430229986144)
XLA Ops:
  0.6 56.9 %shard_map.158 = (bf16[512,256]{1,0:T(8,128)(2,1)}, bf16[512,256]{1,0:T(8,128)(2,1)}) custom-call(bf16[256,512]{1,0:T(8,128)(2,1)} %key_h.1, bf16[256,512]{1,0:T(8,128)(2,1)} %val_h.1, bf16[256,512]{1,0:T(8,128)(2,1)} %qry_h.1, bf16[256,512]{1,0:T(8,128)(2,1)} %gout_h.1, bf16[256,512]{1,0:T(8,128)(2,1)} %filt_h.1, bf16[2048,512]{1,0:T(8,128)(2,1)} %wk_h.1, ...), custom_call_target="tpu_custom_call" | custom-call | tf_op jit(solution)/shard_map/pallas_call | solution.py:279
  57.6 2.1 %shard_map.159 = (bf16[256,512]{1,0:T(8,128)(2,1)}, bf16[256,512]{1,0:T(8,128)(2,1)}) custom-call(bf16[512,256]{1,0:T(8,128)(2,1)} %get-tuple-element.4.gin_t, bf16[512,256]{1,0:T(8,128)(2,1)} %get-tuple-element.5.gfil_t), custom_call_target="tpu_custom_call" | custom-call | tf_op jit(solution)/shard_map/pallas_call | solution.py:310

commit v2 on v1

--- a/solution.py
+++ b/solution.py
@@ -18,6 +18,8 @@
 WIDTH = 512
 D_OUT = 2048
 HALF = 256
+PIECES = 8
+PIECE = WIDTH // PIECES
 
 
 def tables():
@@ -81,6 +83,14 @@
     far = (tp + 2) % 4
     diag = 3 - tp
 
+    barrier = pltpu.get_barrier_semaphore()
+    for t in (sib, far):
+        pl.semaphore_signal(barrier, inc=1, device_id={"tp": t})
+
+    @pl.loop(0, BLOCKS - 1)
+    def _(i):
+        pl.semaphore_signal(barrier, inc=1, device_id={"ctx": partner(me, i)})
+
     pairs = [
         (filt_h, filt), (eye_h, eye), (qry_h, qry), (gout_h, gout), (key_h, key), (val_h, val),
         (fwd1_h, fwd1), (twr_h, twr), (twi_h, twi), (fwd2_h, fwd2), (inv2_h, inv2), (inv1_h, inv1),
@@ -89,14 +99,6 @@
     loads = [pltpu.make_async_copy(s, d, in_sem.at[n]) for n, (s, d) in enumerate(pairs)]
     for load in loads:
         load.start()
-
-    barrier = pltpu.get_barrier_semaphore()
-    for t in (sib, far):
-        pl.semaphore_signal(barrier, inc=1, device_id={"tp": t})
-
-    @pl.loop(0, BLOCKS - 1)
-    def _(i):
-        pl.semaphore_signal(barrier, inc=1, device_id={"ctx": partner(me, i)})
 
     def flip(src, h):
         return dot_nt(eye[...], src[:, pl.ds(h * HALF, HALF)])
@@ -151,7 +153,7 @@
     def forward(n):
         xbuf[...] = get_recv(n).astype(bf16)
 
-        @pl.loop(0, 2)
+        @pl.loop(0, 2, unroll=True)
         def _(i):
             m = pl.multiple_of(i * HALF, HALF)
             rows = pl.ds(m, HALF)
@@ -162,7 +164,7 @@
             spec[n, rows, :] = dot(t, fwd2[...])
 
     def inverse(na, nb, conj, out):
-        @pl.loop(0, 2)
+        @pl.loop(0, 2, unroll=True)
         def _(i):
             m = pl.multiple_of(i * HALF, HALF)
             rows = pl.ds(m, HALF)
@@ -178,7 +180,7 @@
             ubuf[rows, :] = (tr * c + ti * s).astype(bf16)
             ubuf[pl.ds(m + ROWS, HALF), :] = (ti * c - tr * s).astype(bf16)
 
-        @pl.loop(0, 2)
+        @pl.loop(0, 2, unroll=True)
         def _(i):
             m = pl.multiple_of(i * HALF, HALF)
             y = dot(inv1[pl.ds(m, HALF), :], ubuf[...])
@@ -223,7 +225,7 @@
         )
 
     def rows_of(t, h):
-        return pl.ds(pl.multiple_of(t * WIDTH + h * HALF, HALF), HALF)
+        return pl.ds(pl.multiple_of(t * WIDTH + h * PIECE, PIECE), PIECE)
 
     def term(t, h):
         rows = rows_of(t, h)
@@ -231,32 +233,32 @@
 
     arrived(4)
     gbuf[2] = (get_recv(4) * gout_t[...].astype(f32)).astype(bf16)
-    for h in range(2):
+    for h in range(PIECES):
         sib_out[0, h] = term(diag, h).astype(bf16)
         to_sib(0, h).start()
-    for h in range(2):
+    for h in range(PIECES):
         mine = term(far, h)
         to_sib(0, h).wait_recv()
         far_out[h] = (mine + sib_in[0, h].astype(f32)).astype(bf16)
         to_far(h).start()
-    for h in range(2):
+    for h in range(PIECES):
         sib_out[1, h] = term(sib, h).astype(bf16)
         to_sib(1, h).start()
-    for h in range(2):
+    for h in range(PIECES):
         acc[rows_of(tp, h), :] = term(tp, h)
-    for h in range(2):
+    for h in range(PIECES):
         to_sib(1, h).wait_recv()
         acc[rows_of(tp, h), :] += sib_in[1, h].astype(f32)
     arrived(5)
     gfil_ref[...] = get_recv(5).astype(bf16)
-    for h in range(2):
+    for h in range(PIECES):
         to_far(h).wait_recv()
-        gin_ref[pl.ds(h * HALF, HALF), :] = (acc[rows_of(tp, h), :] + far_in[h].astype(f32)).astype(bf16)
+        gin_ref[pl.ds(h * PIECE, PIECE), :] = (acc[rows_of(tp, h), :] + far_in[h].astype(f32)).astype(bf16)
 
     for n in range(6):
         some = send.at[n, pl.ds(0, BLOCKS - 1)]
         pltpu.make_async_copy(some, some, send_sem.at[n]).wait()
-    for h in range(2):
+    for h in range(PIECES):
         to_sib(0, h).wait_send()
         to_sib(1, h).wait_send()
         to_far(h).wait_send()
@@ -293,15 +295,15 @@
             pltpu.VMEM((2 * ROWS, LEN), bf16),
             pltpu.VMEM((3, WIDTH, LEN), bf16),
             pltpu.VMEM((D_OUT, LEN), f32),
-            pltpu.VMEM((2, 2, HALF, LEN), bf16),
-            pltpu.VMEM((2, 2, HALF, LEN), bf16),
-            pltpu.VMEM((2, HALF, LEN), bf16),
-            pltpu.VMEM((2, HALF, LEN), bf16),
+            pltpu.VMEM((2, PIECES, PIECE, LEN), bf16),
+            pltpu.VMEM((2, PIECES, PIECE, LEN), bf16),
+            pltpu.VMEM((PIECES, PIECE, LEN), bf16),
+            pltpu.VMEM((PIECES, PIECE, LEN), bf16),
             dma((15,)),
             dma((6,)),
             dma((6,)),
-            dma((3, 2)),
-            dma((3, 2)),
+            dma((3, PIECES)),
+            dma((3, PIECES)),
         ],
         compiler_params=pltpu.CompilerParams(
             collective_id=1, has_side_effects=True, vmem_limit_bytes=56 * 2**20

time: 59.7 us -> 58.8 us (0.985)
  Pallas kernels: 59 us -> 58 us
    pallas_call x1, Pallas kernels: 56.9 us -> 56 us  [per_device(): pl.pallas_call(kernel, out_shape=(jax.ShapeDtypeStruct((WIDTH, LEN), bf16...]
where the time goes in v2:
time: 58.8 us; the launch traced here: 58.7 us
  Pallas kernels  58 us (99%)
  between operations  0.64 us (1%)
    pallas_call x1, Pallas kernels, per_device(): pl.pallas_call(kernel, out_shape=(jax.ShapeDtypeStruct((WIDTH, LEN), bf16...  56 us
    pallas_call x1, Pallas kernels, per_device(): pl.pallas_call(turn, out_shape=(jax.ShapeDtypeStruct((LEN, WIDTH), bf16),...  2.09 us

profile of v2, /device:TPU:1, one launch (start us, length us, event | category | flops | bytes accessed | tf_op | source)
XLA Modules:
  0.0 58.7 jit_solution(14050273897467332081)
XLA Ops:
  0.6 56.0 %shard_map.158 = (bf16[512,256]{1,0:T(8,128)(2,1)}, bf16[512,256]{1,0:T(8,128)(2,1)}) custom-call(bf16[256,512]{1,0:T(8,128)(2,1)} %key_h.1, bf16[256,512]{1,0:T(8,128)(2,1)} %val_h.1, bf16[256,512]{1,0:T(8,128)(2,1)} %qry_h.1, bf16[256,512]{1,0:T(8,128)(2,1)} %gout_h.1, bf16[256,512]{1,0:T(8,128)(2,1)} %filt_h.1, bf16[2048,512]{1,0:T(8,128)(2,1)} %wk_h.1, ...), custom_call_target="tpu_custom_call" | custom-call | tf_op jit(solution)/shard_map/pallas_call | solution.py:281
  56.6 2.1 %shard_map.159 = (bf16[256,512]{1,0:T(8,128)(2,1)}, bf16[256,512]{1,0:T(8,128)(2,1)}) custom-call(bf16[512,256]{1,0:T(8,128)(2,1)} %get-tuple-element.4.gin_t, bf16[512,256]{1,0:T(8,128)(2,1)} %get-tuple-element.5.gfil_t), custom_call_target="tpu_custom_call" | custom-call | tf_op jit(solution)/shard_map/pallas_call | solution.py:312

commit v3 on v2

--- a/solution.py
+++ b/solution.py
@@ -68,13 +68,13 @@
 def kernel(
     key_h, val_h, qry_h, gout_h, filt_h, wk_h, wq_h, wv_h,
     fwd1_h, fwd2_h, inv2_h, inv1_h, twr_h, twi_h, eye_h,
-    gin_ref, gfil_ref,
+    gin_h, gfil_h,
     key, val, qry, gout, filt, wk, wq, wv,
     fwd1, fwd2, inv2, inv1, twr, twi, eye,
     key_t, val_t, gout_t,
     send, recv, xbuf, spec, ubuf, gbuf, acc,
     sib_out, sib_in, far_out, far_in,
-    in_sem, send_sem, recv_sem, rs_send, rs_recv,
+    gin_ref, gfil_ref, in_sem, send_sem, recv_sem, rs_send, rs_recv, out_sem,
 ):
     me = lax.axis_index("ctx")
     tp = lax.axis_index("tp")
@@ -208,7 +208,7 @@
     gbuf[0] = (back * val_t[...].astype(f32)).astype(bf16)
     gbuf[1] = (back * key_t[...].astype(f32)).astype(bf16)
 
-    @pl.loop(0, D_OUT // HALF)
+    @pl.loop(0, D_OUT // HALF, unroll=4)
     def _(i):
         rows = pl.ds(pl.multiple_of(i * HALF, HALF), HALF)
         acc[rows, :] = dot(wk[rows, :], gbuf[0]) + dot(wv[rows, :], gbuf[1])
@@ -251,9 +251,17 @@
         acc[rows_of(tp, h), :] += sib_in[1, h].astype(f32)
     arrived(5)
     gfil_ref[...] = get_recv(5).astype(bf16)
+    outs = [pltpu.make_async_copy(gfil_ref, gfil_h, out_sem.at[PIECES])]
+    outs[0].start()
     for h in range(PIECES):
         to_far(h).wait_recv()
         gin_ref[pl.ds(h * PIECE, PIECE), :] = (acc[rows_of(tp, h), :] + far_in[h].astype(f32)).astype(bf16)
+        rows = pl.ds(h * PIECE, PIECE)
+        outs.append(pltpu.make_async_copy(gin_ref.at[rows], gin_h.at[rows], out_sem.at[h]))
+        outs[-1].start()
+
+    for out in outs:
+        out.wait()
 
     for n in range(6):
         some = send.at[n, pl.ds(0, BLOCKS - 1)]
@@ -282,7 +290,7 @@
         kernel,
         out_shape=(jax.ShapeDtypeStruct((WIDTH, LEN), bf16),) * 2,
         in_specs=[pl.BlockSpec(memory_space=pl.ANY)] * 15,
-        out_specs=[pl.BlockSpec(memory_space=pltpu.VMEM)] * 2,
+        out_specs=[pl.BlockSpec(memory_space=pl.ANY)] * 2,
         scratch_shapes=[act()] * 5
         + [weight()] * 3
         + [pltpu.VMEM(c.shape, c.dtype) for c in consts]
@@ -299,11 +307,14 @@
             pltpu.VMEM((2, PIECES, PIECE, LEN), bf16),
             pltpu.VMEM((PIECES, PIECE, LEN), bf16),
             pltpu.VMEM((PIECES, PIECE, LEN), bf16),
+            turned(),
+            turned(),
             dma((15,)),
             dma((6,)),
             dma((6,)),
             dma((3, PIECES)),
             dma((3, PIECES)),
+            dma((PIECES + 1,)),
         ],
         compiler_params=pltpu.CompilerParams(
             collective_id=1, has_side_effects=True, vmem_limit_bytes=56 * 2**20

time: 58.8 us -> 58.7 us (level)
  no operation moved by 1% of the time
where the time goes in v3:
time: 58.7 us; the launch traced here: 58.6 us
  Pallas kernels  57.9 us (99%)
  between operations  0.64 us (1%)
    pallas_call x1, Pallas kernels, per_device(): pl.pallas_call(kernel, out_shape=(jax.ShapeDtypeStruct((WIDTH, LEN), bf16...  55.8 us
    pallas_call x1, Pallas kernels, per_device(): pl.pallas_call(turn, out_shape=(jax.ShapeDtypeStruct((LEN, WIDTH), bf16),...  2.08 us

profile of v3, /device:TPU:1, one launch (start us, length us, event | category | flops | bytes accessed | tf_op | source)
XLA Modules:
  0.0 58.6 jit_solution(13192797900913621261)
XLA Ops:
  0.6 55.8 %shard_map.158 = (bf16[512,256]{1,0:T(8,128)(2,1)}, bf16[512,256]{1,0:T(8,128)(2,1)}) custom-call(bf16[256,512]{1,0:T(8,128)(2,1)} %key_h.1, bf16[256,512]{1,0:T(8,128)(2,1)} %val_h.1, bf16[256,512]{1,0:T(8,128)(2,1)} %qry_h.1, bf16[256,512]{1,0:T(8,128)(2,1)} %gout_h.1, bf16[256,512]{1,0:T(8,128)(2,1)} %filt_h.1, bf16[2048,512]{1,0:T(8,128)(2,1)} %wk_h.1, ...), custom_call_target="tpu_custom_call" | custom-call | tf_op jit(solution)/shard_map/pallas_call | solution.py:289
  56.5 2.1 %shard_map.159 = (bf16[256,512]{1,0:T(8,128)(2,1)}, bf16[256,512]{1,0:T(8,128)(2,1)}) custom-call(bf16[512,256]{1,0:T(8,128)(2,1)} %get-tuple-element.4.gin_t, bf16[512,256]{1,0:T(8,128)(2,1)} %get-tuple-element.5.gfil_t), custom_call_target="tpu_custom_call" | custom-call | tf_op jit(solution)/shard_map/pallas_call | solution.py:323
